TPU v7x, 256 devices: a whole 4x4x8 slice. The times are simulated.
256 devices in a mesh: dp: 32 (over x_lo, z, core), expert: 8 (over x_hi, y).
Axes of the slice: x: 4 (x_hi: 2, x_lo: 2; x = x_hi * 2 + x_lo), y: 4, z: 8, core: 2. Of those that a mesh axis runs over, the one named last changes fastest.
Arguments:
- tokens: bfloat16 [49152, 4096], P(('dp', 'expert')), may hold values from -24 to 24
- routes: int32 [49152, 2], P(('dp', 'expert')), may hold values from 0 to 7, all different within a row; in each aligned block of 192 rows (0 to 191, 192 to 383, ...) at most 64 rows name the same one
- positives: int32 [512], P(('dp', 'expert')), may hold values from 0 to 511, each once
- expert_out: bfloat16 [32, 8, 8, 64, 4096], P('dp', 'expert'), may hold values from -6 to 6
- router: bfloat16 [4096, 8], replicated, may hold values from -0.09375 to 0.09375
- norm_gain: float32 [4096], replicated, may hold values from 0.25 to 1.75
- loss_scale: float32 [], replicated, may hold values from 8192 to 65536
Outputs:
- token_grad: bfloat16 [49152, 4096], P(('dp', 'expert'))
- expert_grad: bfloat16 [32, 8, 8, 64, 4096], P('dp', 'expert')
- router_grad: float32 [4096, 8], replicated
- loss: float32 [], replicated
Inputs may be any that keep to these rules, and one draw needn't show every extreme that they name: `routes`: each row names 2 different experts; among the rows of one device no expert is named by more than 64 rows, a bound that some block reaches. `positives`: A permutation of the records.
All inputs are finite; a program needn't handle non-finite values.
Results may differ from a plain program's by a relative error of at most 0.0061.
Values may be sent and summed in bfloat16 or wider, within the bound.
No kernel may reach another device: no remote copies, remote signals or barrier semaphores. Data moves between devices by JAX's collectives and lax.ppermute only.
A program may use at most 128 MiB of HBM per device.

v0:
```python
import math
import jax
import jax.numpy as jnp
from jax import lax
from jax.sharding import PartitionSpec as P

PAIR_DEV = 2
SEQ = 48
norm_eps = 1e-05


def slot_where(routes, experts, capacity):
    hit_table = (routes[:, :, None] == jnp.arange(experts, dtype=jnp.int32)[None, None, :]).astype(
        jnp.int32
    )
    flat_hits = hit_table.reshape(-1, experts)
    before = jnp.cumsum(flat_hits, axis=0) - flat_hits
    slot_rank = jnp.sum(before * flat_hits, axis=1).reshape(routes.shape)
    return routes * capacity + slot_rank


def forward_rows(tokens, routes, received, router, norm_gain):
    experts = received.shape[0]
    capacity = received.shape[1]
    hidden_width = received.shape[2]
    logits = jnp.dot(tokens, router, preferred_element_type=jnp.float32)
    one_hot = (routes[:, :, None] == jnp.arange(experts, dtype=jnp.int32)[None, None, :]).astype(
        jnp.float32
    )
    chosen = jnp.sum(one_hot * logits[:, None, :], axis=2)
    gate_mix = jax.nn.softmax(chosen, axis=1)
    slot_rows = slot_where(routes, experts, capacity)
    fetched = received.reshape(experts * capacity, hidden_width)[slot_rows]
    summed_rows = (
        tokens.astype(jnp.float32)
        + gate_mix[:, 0:1] * fetched[:, 0].astype(jnp.float32)
        + gate_mix[:, 1:2] * fetched[:, 1].astype(jnp.float32)
    )
    inverse = lax.rsqrt(jnp.mean(summed_rows * summed_rows, axis=1, keepdims=True) + norm_eps)
    normed = summed_rows * inverse * norm_gain
    pooled = jnp.mean(normed.reshape(-1, SEQ, hidden_width), axis=1).astype(jnp.bfloat16)
    return (pooled, (gate_mix, one_hot, slot_rows, fetched, summed_rows, inverse))


def backward_rows(tokens, router, norm_gain, saved, grad_pool, experts, capacity):
    gate_mix, one_hot, slot_rows, fetched, summed_rows, inverse = saved
    hidden_width = tokens.shape[1]
    grad_rows = jnp.broadcast_to(
        grad_pool[:, None, :] / SEQ, (grad_pool.shape[0], SEQ, hidden_width)
    ).reshape(-1, hidden_width)
    weighted = grad_rows * norm_gain
    grad_summed = inverse * weighted - summed_rows * inverse**3 * jnp.mean(
        weighted * summed_rows, axis=1, keepdims=True
    )
    grad_gate = jnp.sum(grad_summed[:, None, :] * fetched.astype(jnp.float32), axis=2)
    grad_chosen = gate_mix * (grad_gate - jnp.sum(gate_mix * grad_gate, axis=1, keepdims=True))
    grad_logits = jnp.sum(one_hot * grad_chosen[:, :, None], axis=1).astype(jnp.bfloat16)
    router_part = lax.dot_general(
        tokens, grad_logits, (((0,), (0,)), ((), ())), preferred_element_type=jnp.float32
    )
    through_router = lax.dot_general(
        grad_logits, router, (((1,), (1,)), ((), ())), preferred_element_type=jnp.float32
    )
    token_grad = (grad_summed + through_router).astype(jnp.bfloat16)
    outgoing = (
        (gate_mix[:, :, None] * grad_summed[:, None, :])
        .astype(jnp.bfloat16)
        .reshape(-1, hidden_width)
    )
    sendback = (
        jnp.zeros((experts * capacity, hidden_width), jnp.bfloat16)
        .at[slot_rows.reshape(-1)]
        .set(outgoing)
    )
    return (token_grad, sendback.reshape(experts, capacity, hidden_width), router_part)


def score_rows(queries, records_all, positives, loss_scale, pair_total, score_scale):
    scores = (
        lax.dot_general(
            queries, records_all, (((1,), (1,)), ((), ())), preferred_element_type=jnp.float32
        )
        * score_scale
    )
    highest = jnp.max(scores, axis=1, keepdims=True)
    log_total = highest[:, 0] + jnp.log(jnp.sum(jnp.exp(scores - highest), axis=1))
    is_positive = jnp.arange(pair_total, dtype=jnp.int32)[None, :] == positives[:, None]
    positive_score = jnp.sum(jnp.where(is_positive, scores, jnp.zeros_like(scores)), axis=1)
    row_loss = log_total - positive_score
    softmax_rows = jnp.exp(scores - log_total[:, None])
    score_grad = (
        (softmax_rows - is_positive.astype(jnp.float32)) * (loss_scale / pair_total)
    ).astype(jnp.bfloat16)
    return (row_loss, score_grad)


def shards(tokens, routes, positives, expert_out, router, norm_gain, loss_scale):
    experts = expert_out.shape[2]
    capacity = expert_out.shape[3]
    hidden_width = expert_out.shape[4]
    received = lax.all_to_all(
        expert_out.reshape(experts, capacity, hidden_width),
        "expert",
        split_axis=0,
        concat_axis=0,
        tiled=True,
    )
    pooled, saved = forward_rows(tokens, routes, received, router, norm_gain)
    queries = pooled[:PAIR_DEV]
    records = pooled[PAIR_DEV:]
    loop_size = lax.axis_size("dp")
    column_size = lax.axis_size("expert")
    device_count = loop_size * column_size
    pair_total = PAIR_DEV * device_count
    score_scale = 4.0 / math.sqrt(hidden_width)
    records_all = lax.all_gather(records, ("dp", "expert"), axis=0, tiled=True)
    row_loss, score_grad = score_rows(
        queries, records_all, positives, loss_scale, pair_total, score_scale
    )
    loss_local = jnp.sum(row_loss)
    grad_queries = (
        jnp.dot(score_grad, records_all, preferred_element_type=jnp.float32) * score_scale
    )
    grad_records = lax.psum_scatter(
        lax.dot_general(
            score_grad, queries, (((0,), (0,)), ((), ())), preferred_element_type=jnp.float32
        )
        * score_scale,
        ("dp", "expert"),
        scatter_dimension=0,
        tiled=True,
    )
    grad_pool = jnp.concatenate([grad_queries, grad_records], axis=0)
    token_grad, sendback, router_part = backward_rows(
        tokens, router, norm_gain, saved, grad_pool, experts, capacity
    )
    returned = lax.all_to_all(sendback, "expert", split_axis=0, concat_axis=0, tiled=True)
    router_grad, loss_total = lax.psum((router_part, loss_local), ("dp", "expert"))
    expert_grad = returned.reshape(1, 1, experts, capacity, hidden_width)
    return (token_grad, expert_grad, router_grad, loss_total / pair_total)


def solution(mesh):
    placed = (
        P(("dp", "expert"), None),
        P(("dp", "expert"), None),
        P(("dp", "expert")),
        P("dp", "expert", None, None, None),
        P(),
        P(),
        P(),
    )
    return jax.shard_map(
        shards,
        mesh=mesh,
        in_specs=placed,
        out_specs=(P(("dp", "expert"), None), P("dp", "expert", None, None, None), P(), P()),
        check_vma=False,
    )
```

profile of v0, /device:TPU:8, one launch (start us, length us, event | category | flops | bytes accessed | tf_op | source)
XLA Modules:
  0.0 1506.5 jit_solution(1943185011051784695)
XLA Ops:
  7.2 7.5 all-to-all-start
  14.7 0.1 copy.45
  14.9 0.1 eq.59
  15.0 0.1 eq.55
  15.2 0.9 reduce-window.6
  16.0 0.2 slice_reduce_fusion
  16.4 0.1 reshape.211
  16.6 0.1 copy.48
  16.8 0.1 reshape.221
  16.9 0.5 fusion.20
  17.5 45.7 %all-to-all-done = bf16[8,64,4096]{2,1,0:T(8,128)(2,1)} async-done(((bf16[8,64,4096]{2,1,0:T(8,128)(2,1)}), bf16[8,64,4096]{2,1,0:T(8,128)(2,1)}, u32[]{:S(2)}, u32[]{:S(2)}) %all-to-all-start) | async-done | bytes 4194336 | tf_op jit(solution)/shard_map/all_to_all | solution.py:101
  63.2 11.0 gather_fusion
  74.2 4.6 reshape.220
  78.8 7.0 fusion.17
  85.8 4.0 multiply_reduce_fusion.2
  89.9 2.4 multiply_multiply_fusion
  92.3 0.2 copy-done.2
  92.5 2.2 reduce_sum.112
  94.7 0.6 slice_bitcast_fusion
  95.3 0.2 all-reduce.6.cloned.1.call-start
  96.2 680.8 %all-gather.3.cloned.1.call-done = bf16[256,2,4096]{2,1,0:T(2,128)(2,1)} async-done(((bf16[1,2,4096]{2,1,0:T(2,128)(2,1)}), bf16[256,2,4096]{2,1,0:T(2,128)(2,1)}) %all-gather.3.cloned.1.call-update) | async-done | bytes 4194320 | tf_op jit(solution)/shard_map/all_gather | solution.py:116
  777.0 7.2 reshape.238
  784.2 3.5 fusion.19
  787.7 0.2 select_reduce_fusion.2
  787.9 0.6 subtract_reduce_fusion
  788.5 4.6 convolution_multiply_fusion
  793.3 0.1 div.48
  793.4 0.1 copy.53
  793.5 0.1 reshape.214
  793.7 2.9 convolution_multiply_fusion.1
  796.6 301.1 %all-reduce.6.cloned.1.call-done = f32[512,4096]{1,0:T(8,128)} async-done(((f32[512,4096]{1,0:T(8,128)}), f32[512,4096]{1,0:T(8,128)}) %all-reduce.6.cloned.1.call-update) | async-done | bytes 8388624
  1097.7 1.1 constant_dynamic-slice_fusion
  1098.8 0.3 bitcast_multiply_fusion
  1099.2 0.5 copy-done.3
  1099.7 0.4 multiply_reduce_fusion.1
  1100.1 0.7 multiply_subtract_fusion
  1100.8 1.7 copy-done.1
  1102.5 5.3 mul.182
  1107.8 8.4 mul.189
  1116.2 9.7 scatter_custom_fusion
  1125.9 6.8 all-to-all-start.1
  1132.6 112.4 %psum.15 = f32[]{:T(128)} all-reduce(f32[]{:T(128)} %get-tuple-element.6), channel_id=1, replica_groups=mesh['dp'=32,'expert'=8] {'dp','expert'}, use_global_device_ids=true, to_apply=%region_19.20 | all-reduce | flops 1 | bytes 8 | tf_op jit(solution)/shard_map/psum | solution.py:138
  1245.7 5.7 multiply_reduce_fusion
  1251.5 2.4 convolution_bitcast_fusion
  1254.0 3.6 fusion
  1257.6 235.8 %all-reduce.4.cloned.1.call-done = f32[4096,8]{0,1:T(8,128)} async-done(((f32[4096,8]{0,1:T(8,128)}), f32[4096,8]{0,1:T(8,128)}) %all-reduce.4.cloned.1.call-update) | async-done | bytes 131088 | tf_op jit(solution)/shard_map/psum | solution.py:138
  1493.4 4.7 copy.69
  1498.2 0.7 copy.70
  (44 shorter events, 0.8 us)
Async XLA Ops:
  7.2 9.7 copy-start
  7.2 7.5 copy-start.8
  7.2 9.7 copy-start.4
  7.2 56.0 %all-to-all-start = ((bf16[8,64,4096]{2,1,0:T(8,128)(2,1)}), bf16[8,64,4096]{2,1,0:T(8,128)(2,1)}, u32[]{:S(2)}, u32[]{:S(2)}) async-start(bf16[8,64,4096]{2,1,0:T(8,128)(2,1)} %bitcast.46), calls=%async_computation | async-start | bytes 8388608 | tf_op jit(solution)/shard_map/all_to_all | solution.py:101
  14.7 762.3 %all-gather.3.cloned.1.call-start = ((), (), s32[]{:S(2)}) async-start(), calls=%async_computation.3 | async-start | bytes 4210688 | tf_op jit(solution)/shard_map/all_gather | solution.py:116
  78.8 7.0 copy-start.5
  85.8 4.1 copy-start.6
  89.8 2.6 copy-start.2
  95.3 1002.4 %all-reduce.6.cloned.1.call-start = ((), (), s32[]{:S(2)}) async-start(), calls=%async_computation.4 | async-start | bytes 16777216
  784.2 3.5 copy-start.9
  1097.7 2.0 copy-start.3
  1100.8 1.7 copy-start.1
  1125.9 131.7 %all-to-all-start.1 = ((bf16[8,64,4096]{2,1,0:T(8,128)(2,1)}), bf16[8,64,4096]{2,1,0:T(8,128)(2,1)}, u32[]{:S(2)}, u32[]{:S(2)}) async-start(bf16[8,64,4096]{2,1,0:T(8,128)(2,1)} %bitcast.44), calls=%async_computation.1 | async-start | bytes 8388608 | tf_op jit(solution)/shard_map/all_to_all | solution.py:137
  1132.6 360.8 %all-reduce.4.cloned.1.call-start = ((), (), s32[]{:S(2)}) async-start(), calls=%async_computation.2 | async-start | bytes 262144 | tf_op jit(solution)/shard_map/psum | solution.py:138
  1493.4 4.7 copy-start.7
Sparse Core Ops, SparseCore 0:
  95.4 681.5 all-gather.2
  793.3 304.4 all-reduce.5
  1254.1 239.3 all-reduce.3
where the time goes:
time: 1510 us
  waiting for transfers between devices  1260 us (83%)
  blocking collectives  112 us (7%)
  local copies, waits for them, and re-layouts  54.7 us (4%)
  other arithmetic  27.5 us (2%)
  matrix products  17.5 us (1%)
  between operations  16.5 us (1%)
    all_gather x1, waiting for transfers between devices, shards(): records_all = lax.all_gather(records, ('dp', 'expert'), axis=0, tiled=True)  681 us
    unnamed x4, waiting for transfers between devices  301 us
    psum x1, waiting for transfers between devices, shards(): lax.psum((router_part, loss_local), ('dp', 'expert'))  236 us
    psum x1, blocking collectives, shards(): lax.psum((router_part, loss_local), ('dp', 'expert'))  112 us
    all_to_all x1, waiting for transfers between devices, shards(): lax.all_to_all(expert_out.reshape(experts, capacity, hidden_width), 'expe...  45.7 us
  transfers between devices with their start and end apart: 5, of which 4 were waited for; matrix products, arithmetic and copies ran while one was open for 1% of the time, Pallas kernels for 0%

commit v1 on v0

--- a/solution.py
+++ b/solution.py
@@ -113,7 +113,12 @@
     device_count = loop_size * column_size
     pair_total = PAIR_DEV * device_count
     score_scale = 4.0 / math.sqrt(hidden_width)
-    records_all = lax.all_gather(records, ("dp", "expert"), axis=0, tiled=True)
+    records_all = jnp.concatenate(
+        lax.all_to_all(
+            jnp.stack([records] * lax.axis_size(("dp", "expert"))), ("dp", "expert"), 0, 0
+        ),
+        axis=0,
+    )
     row_loss, score_grad = score_rows(
         queries, records_all, positives, loss_scale, pair_total, score_scale
     )

time: 1510 us -> 912 us (0.60)
  waiting for transfers between devices: 1260 us -> 648 us
    all_gather x1 -> x0, waiting for transfers between devices: 681 us -> none  [shards(): records_all = lax.all_gather(records, ('dp', 'expert'), axis=0, tiled=True)]
    all_to_all x0 -> x1, waiting for transfers between devices: none -> 94.9 us  [shards(): lax.all_to_all(jnp.stack([records] * lax.axis_size(('dp', 'expert'))), ('...]
    unnamed x4 -> x3, waiting for transfers between devices: 301 us -> 272 us
  transfers between devices with their start and end apart: 5 -> 5, of which waited for: 4 -> 4; matrix products, arithmetic and copies ran while one was open for 1% -> 2% of each run, Pallas kernels for 0% -> 0%
where the time goes in v1:
time: 912 us; the launch traced here: 910 us
  waiting for transfers between devices  648 us (71%)
  blocking collectives  112 us (12%)
  local copies, waits for them, and re-layouts  60.5 us (7%)
  starting transfers between devices  27.8 us (3%)
  other arithmetic  27.5 us (3%)
  matrix products  17.5 us (2%)
  between operations  16.8 us (2%)
    unnamed x3, waiting for transfers between devices  272 us
    psum x1, waiting for transfers between devices, shards(): lax.psum((router_part, loss_local), ('dp', 'expert'))  236 us
    psum x1, blocking collectives, shards(): lax.psum((router_part, loss_local), ('dp', 'expert'))  112 us
    all_to_all x1, waiting for transfers between devices, shards(): lax.all_to_all(jnp.stack([records] * lax.axis_size(('dp', 'expert'))), ('...  94.9 us
    all_to_all x1, waiting for transfers between devices, shards(): lax.all_to_all(expert_out.reshape(experts, capacity, hidden_width), 'expe...  45.7 us
  transfers between devices with their start and end apart: 5, of which 4 were waited for; matrix products, arithmetic and copies ran while one was open for 2% of the time, Pallas kernels for 0%

profile of v1, /device:TPU:8, one launch (start us, length us, event | category | flops | bytes accessed | tf_op | source)
XLA Modules:
  0.0 910.4 jit_solution(16754102881701877243)
XLA Ops:
  7.2 7.5 all-to-all-start
  14.8 0.1 eq.59
  15.0 0.1 eq.55
  15.2 0.9 reduce-window.6
  16.0 0.2 slice_reduce_fusion
  16.4 0.1 reshape.216
  16.6 0.1 copy.48
  16.7 0.1 reshape.227
  16.9 0.5 fusion.20
  17.5 45.7 %all-to-all-done = bf16[8,64,4096]{2,1,0:T(8,128)(2,1)} async-done(((bf16[8,64,4096]{2,1,0:T(8,128)(2,1)}), bf16[8,64,4096]{2,1,0:T(8,128)(2,1)}, u32[]{:S(2)}, u32[]{:S(2)}) %all-to-all-start) | async-done | bytes 4194336 | tf_op jit(solution)/shard_map/all_to_all | solution.py:101
  63.2 11.0 %gather_fusion = bf16[384,4096]{1,0:T(8,128)(2,1)} fusion(bf16[512,4096]{1,0:T(8,128)(2,1)} %bitcast.2, s32[1024]{0:T(1024)S(1)} %pad_clamp_fusion), kind=kCustom, calls=%fused_computation | custom fusion | bytes 6292992 | tf_op jit(solution)/shard_map/gather | solution.py:33
  74.2 4.6 reshape.226
  78.8 7.2 fusion.17
  86.0 4.0 multiply_reduce_fusion.2
  90.0 2.4 multiply_multiply_fusion
  92.4 0.2 copy-done.2
  92.6 2.2 reduce_sum.112
  94.9 6.3 stack.2
  101.1 13.5 %all-to-all-start.1 = ((bf16[256,2,4096]{2,1,0:T(2,128)(2,1)}), bf16[256,2,4096]{2,1,0:T(2,128)(2,1)}, u32[]{:S(2)}, u32[]{:S(2)}) async-start(bf16[256,2,4096]{2,1,0:T(2,128)(2,1)} %stack.2), calls=%async_computation.1 | async-start | bytes 8388608 | tf_op jit(solution)/shard_map/all_to_all | solution.py:117
  115.4 94.9 %all-to-all-done.1 = bf16[256,2,4096]{2,1,0:T(2,128)(2,1)} async-done(((bf16[256,2,4096]{2,1,0:T(2,128)(2,1)}), bf16[256,2,4096]{2,1,0:T(2,128)(2,1)}, u32[]{:S(2)}, u32[]{:S(2)}) %all-to-all-start.1) | async-done | bytes 4194336 | tf_op jit(solution)/shard_map/all_to_all | solution.py:117
  210.3 7.2 reshape.218
  217.4 3.5 fusion.19
  221.0 0.2 select_reduce_fusion.2
  221.2 0.6 subtract_reduce_fusion
  221.8 4.6 convolution_multiply_fusion
  226.4 0.1 copy.54
  226.5 0.1 div.48
  226.7 0.1 copy.53
  226.8 0.1 reshape.220
  227.0 2.9 convolution_multiply_fusion.1
  229.9 271.5 %all-reduce.6.cloned.1.call-done = f32[512,4096]{1,0:T(8,128)} async-done(((f32[512,4096]{1,0:T(8,128)}), f32[512,4096]{1,0:T(8,128)}) %all-reduce.6.cloned.1.call-update) | async-done | bytes 8388624
  501.4 1.1 constant_dynamic-slice_fusion
  502.5 0.3 bitcast_multiply_fusion
  502.9 0.5 copy-done.3
  503.3 0.4 multiply_reduce_fusion.1
  503.7 0.7 multiply_subtract_fusion
  504.5 1.7 copy-done.1
  506.1 5.3 mul.182
  511.4 8.4 mul.189
  519.9 9.7 %scatter_custom_fusion = bf16[512,4096]{1,0:T(8,128)(2,1)} fusion(s32[384]{0:T(512)S(1)} %fusion.13, f32[384,4096]{1,0:T(8,128)} %mul.189, f32[384]{0:T(512)S(1)} %div.48, bf16[]{:T(256)} %constant.41.clone.1), kind=kCustom, calls=%fused_computation.9 | custom fusion | flops 3145728 | bytes 10487810 | tf_op jit(solution)/shard_map/scatter | solution.py:73
  529.5 6.8 all-to-all-start.2
  536.3 112.4 %psum.15 = f32[]{:T(128)} all-reduce(f32[]{:T(128)} %get-tuple-element.6), channel_id=1, replica_groups=mesh['dp'=32,'expert'=8] {'dp','expert'}, use_global_device_ids=true, to_apply=%region_19.20 | all-reduce | flops 1 | bytes 8 | tf_op jit(solution)/shard_map/psum | solution.py:143
  649.3 5.7 multiply_reduce_fusion
  655.2 2.4 convolution_bitcast_fusion
  657.6 3.6 fusion
  661.3 235.8 %all-reduce.4.cloned.1.call-done = f32[4096,8]{0,1:T(8,128)} async-done(((f32[4096,8]{0,1:T(8,128)}), f32[4096,8]{0,1:T(8,128)}) %all-reduce.4.cloned.1.call-update) | async-done | bytes 131088 | tf_op jit(solution)/shard_map/psum | solution.py:143
  897.1 4.7 copy.69
  901.8 0.7 copy.70
  (44 shorter events, 0.8 us)
Async XLA Ops:
  7.2 9.7 %copy-start = (bf16[4096,8]{0,1:T(8,128)(2,1)S(1)}, bf16[4096,8]{0,1:T(8,128)(2,1)}, u32[]{:S(2)}) copy-start(bf16[4096,8]{0,1:T(8,128)(2,1)} %param.11) | copy-start | bytes 196612
  7.2 7.5 copy-start.8
  7.2 9.7 %copy-start.4 = (bf16[192,4096]{1,0:T(8,128)(2,1)S(1)}, bf16[192,4096]{1,0:T(8,128)(2,1)}, u32[]{:S(2)}) copy-start(bf16[192,4096]{1,0:T(8,128)(2,1)} %param.7) | copy-start | bytes 4718596
  7.2 56.0 %all-to-all-start = ((bf16[8,64,4096]{2,1,0:T(8,128)(2,1)}), bf16[8,64,4096]{2,1,0:T(8,128)(2,1)}, u32[]{:S(2)}, u32[]{:S(2)}) async-start(bf16[8,64,4096]{2,1,0:T(8,128)(2,1)} %bitcast.44), calls=%async_computation | async-start | bytes 8388608 | tf_op jit(solution)/shard_map/all_to_all | solution.py:101
  78.8 7.2 copy-start.5
  86.0 4.1 copy-start.6
  90.0 2.6 copy-start.2
  101.1 109.1 %all-to-all-start.1 = ((bf16[256,2,4096]{2,1,0:T(2,128)(2,1)}), bf16[256,2,4096]{2,1,0:T(2,128)(2,1)}, u32[]{:S(2)}, u32[]{:S(2)}) async-start(bf16[256,2,4096]{2,1,0:T(2,128)(2,1)} %stack.2), calls=%async_computation.1 | async-start | bytes 8388608 | tf_op jit(solution)/shard_map/all_to_all | solution.py:117
  114.7 386.7 %all-reduce.6.cloned.1.call-start = ((), (), s32[]{:S(2)}) async-start(), calls=%async_computation.4 | async-start | bytes 16777216
  217.4 3.5 copy-start.9
  501.4 2.0 copy-start.3
  504.5 1.7 copy-start.1
  529.5 131.7 %all-to-all-start.2 = ((bf16[8,64,4096]{2,1,0:T(8,128)(2,1)}), bf16[8,64,4096]{2,1,0:T(8,128)(2,1)}, u32[]{:S(2)}, u32[]{:S(2)}) async-start(bf16[8,64,4096]{2,1,0:T(8,128)(2,1)} %bitcast.42), calls=%async_computation.2 | async-start | bytes 8388608 | tf_op jit(solution)/shard_map/all_to_all | solution.py:142
  536.3 360.8 %all-reduce.4.cloned.1.call-start = ((), (), s32[]{:S(2)}) async-start(), calls=%async_computation.3 | async-start | bytes 262144 | tf_op jit(solution)/shard_map/psum | solution.py:143
  897.1 4.7 copy-start.7
Sparse Core Ops, SparseCore 0:
  226.5 274.8 all-reduce.5
  657.7 239.3 all-reduce.3
